TPU v7x, 32 devices: a whole 2x2x4 slice. The times are simulated.
32 devices in a mesh: cand: 4 (over x, core), seq: 8 (over z, y).
Axes of the slice: x: 2, y: 2, z: 4, core: 2. Of those that a mesh axis runs over, the one named last changes fastest.
Arguments:
- response_query_array: bfloat16 [8, 768, 2560], P('cand', 'seq'), may hold values from -180 to 180
- response_key_array: bfloat16 [8, 768, 512], P('cand', 'seq'), may hold values from -6 to 6
- response_value_array: bfloat16 [8, 768, 512], P('cand', 'seq'), may hold values from -6 to 6
- prompt_key_array: bfloat16 [2048, 512], P(('cand', 'seq')), may hold values from -6 to 6
- prompt_value_array: bfloat16 [2048, 512], P(('cand', 'seq')), may hold values from -6 to 6
- lengths: int32 [8], replicated, may hold values from 192 to 768, as said below
- offsets: int32 [8], replicated, may hold values from 512 to 2048, as said below
- ranks: int32 [8], replicated, may hold values from 0 to 7, each once
Outputs:
- attention: bfloat16 [8, 768, 2560], P('cand', 'seq')
Inputs may be any that keep to these rules, and one draw needn't show every extreme that they name: `lengths`: some candidate's response has all 768 positions live. `offsets`: some candidate sees the whole prompt.
All inputs are finite; a program needn't handle non-finite values.
Results may differ from a plain program's by a relative error of at most 0.004.
Values may be sent and summed in bfloat16 or wider, within the bound.
No kernel may reach another device: no remote copies, remote signals or barrier semaphores. Data moves between devices by JAX's collectives and lax.ppermute only.
A program may use at most 128 MiB of HBM per device.

v0:
```python
import functools
import math

import jax
import jax.numpy as jnp
from jax import lax
from jax.experimental import pallas as pl
from jax.experimental.pallas import tpu as pltpu
from jax.sharding import PartitionSpec as P

QUERY_HEADS = 20
KEY_VALUE_HEADS = 4
HEAD = 128
GROUP = QUERY_HEADS // KEY_VALUE_HEADS
WIDE = GROUP * HEAD
SCORE_FACTOR = math.log2(math.e) / math.sqrt(HEAD)
LOWEST = -1e30
AXES = ("cand", "seq")
PACK_VMEM = 60 << 20
VMEM = pl.BlockSpec(memory_space=pltpu.VMEM)
SMEM = pl.BlockSpec(memory_space=pltpu.SMEM)


class Layout:
    def __init__(self, mesh):
        assert mesh.shape["cand"] == 4 and mesh.shape["seq"] % 2 == 0
        self.rings = mesh.shape["seq"] // 2

    def permute(self, array, d=0, core=0, ring=0):
        pairs = []
        for x in range(2):
            for c in range(2):
                for r in range(self.rings):
                    for y in range(2):
                        source = ((x * 2 + c) * self.rings + r) * 2 + y
                        target = ((x ^ (d >> 1)) * 2 + (c ^ core)) * self.rings
                        target = (target + (r + ring) % self.rings) * 2 + (y ^ (d & 1))
                        pairs.append((source, target))
        return lax.ppermute(array, AXES, pairs)

    def exchange(self, pieces):
        return [pieces[0]] + [self.permute(pieces[d], d=d) for d in range(1, 4)]

    def spread(self, block):
        return [block] + [self.permute(block, ring=k) for k in range(1, self.rings)]

    def ring_gather(self, block):
        pieces = [block]
        for _ in range(self.rings - 1):
            pieces.append(self.permute(pieces[-1], ring=1))
        return pieces


def kernel_call(kernel, out_shape, operands, scratch=(), cost=(0, 0), name=None, scalars=1, spare=2 << 20):
    many = isinstance(out_shape, list)
    arrays = list(operands) + (list(out_shape) if many else [out_shape]) + list(scratch)
    held = sum(math.prod(a.shape) * jnp.dtype(a.dtype).itemsize for a in arrays)
    return pl.pallas_call(
        kernel,
        out_shape=out_shape,
        in_specs=[SMEM] * scalars + [VMEM] * (len(operands) - scalars),
        out_specs=[VMEM] * len(out_shape) if many else VMEM,
        scratch_shapes=list(scratch),
        compiler_params=pltpu.CompilerParams(vmem_limit_bytes=held + held // 4 + spare),
        cost_estimate=pl.CostEstimate(
            flops=cost[0], transcendentals=cost[0] // 512, bytes_accessed=cost[1]
        ),
        name=name,
    )(*operands)


def own_head():
    return lax.axis_index("cand") // 2 * 2 + lax.axis_index("seq") % 2


def pack_first_kernel(rk, rv, pk, pv, *refs):
    outs, joined, sems = refs[:4], refs[4], refs[5]
    own = own_head()
    cands, rows = rk.shape[0], rk.shape[1]
    moves = []
    width = pk.shape[1]
    for half, source in enumerate((pk, pv)):
        moves.append((source, joined.at[:, pl.ds(half * width, width)]))
    for d, out in enumerate(outs):
        lane = pl.ds(pl.multiple_of((own ^ d) * HEAD, HEAD), HEAD)
        for half, source in enumerate((rk, rv)):
            for w in range(cands):
                target = out.at[pl.ds(w * rows, rows), pl.ds(half * HEAD, HEAD)]
                moves.append((source.at[w, :, lane], target))
    copies = [pltpu.make_async_copy(a, b, sems.at[n]) for n, (a, b) in enumerate(moves)]
    for copy in copies:
        copy.start()
    for copy in copies:
        copy.wait()


def pack_queries_kernel(q, *outs):
    own = own_head()
    cands, rows = q.shape[0], q.shape[1]
    for d, out in enumerate(outs):
        for w in range(cands):
            for g in range(GROUP):
                lane = pl.multiple_of((own ^ d) * WIDE + g * HEAD, HEAD)
                at = (w * GROUP + g) * rows
                out[at : at + rows, :] = q[w, :, pl.ds(lane, HEAD)]


def pack_kernel(rings, *refs):
    asked, mine, pieces, outs = refs[:4], refs[4:6], refs[6 : 5 + rings], refs[5 + rings :]
    own = own_head()
    rows, width = pieces[0].shape
    for d, out in enumerate(outs):
        first = asked[d].shape[0]
        out[:first, :] = asked[d][...]
        for half in range(2):
            lane = pl.multiple_of((own ^ d) * HEAD + half * (width // 2), HEAD)
            at = first + half * rings * rows
            mine_lane = pl.ds(pl.multiple_of((own ^ d) * HEAD, HEAD), HEAD)
            out[at : at + rows, :] = mine[half][:, mine_lane]
            for k, piece in enumerate(pieces):
                at = first + (half * rings + k + 1) * rows
                out[at : at + rows, :] = piece[:, pl.ds(lane, HEAD)]


def stack_kernel(*refs):
    for n, piece in enumerate(refs[:-1]):
        refs[-1][n] = piece[...]


def unit_facts(facts, w, dx):
    group, count = lax.axis_index("cand"), facts.shape[0] // 3
    x, core = group // 2, group % 2
    cands = count // 4
    rank = ((x ^ dx) * 2 + core) * cands + w
    source = jnp.int32(0)
    for c in range(count):
        source = jnp.where(facts[2 * count + c] == rank, c, source)
    home = source // cands
    away = (home % 2) ^ core
    return away, (home // 2) ^ x, source % cands, facts[source], facts[count + source]


def fetch(unit, dy, own, other, row, rows):
    d = unit[1] * 2 + dy
    at = pl.ds(pl.multiple_of(row, rows), rows)
    return jnp.where(unit[0] == 1, other[d, at, :], own[d, at, :])


def select_keys_kernel(facts, own, other, *outs):
    rows = outs[0].shape[2]
    for w, out in enumerate(outs):
        for dx in range(2):
            unit = unit_facts(facts, w, dx)
            for dy in range(2):
                out[dx, dy] = fetch(unit, dy, own, other, unit[2] * rows, rows)


def load_queries(unit, own, other, q_all):
    rows = q_all.shape[0] // (2 * GROUP)
    for dy in range(2):
        for g in range(GROUP):
            row = (unit[2] * GROUP + g) * rows
            at = (g * 2 + dy) * rows
            q_all[at : at + rows, :] = fetch(unit, dy, own, other, row, rows)


def online_step(q, k, v, mask, state):
    top, total, mixed = state
    scores = lax.dot_general(k, q, (((1,), (1,)), ((), ())), preferred_element_type=jnp.float32)
    scores = scores * SCORE_FACTOR
    if mask is not None:
        scores = jnp.where(mask, scores, LOWEST)
    new_top = jnp.maximum(top, jnp.max(scores, axis=0, keepdims=True))
    scale = jnp.exp2(top - new_top)
    weights = jnp.exp2(scores - new_top)
    total = total * scale + jnp.sum(weights, axis=0, keepdims=True)
    mixed = mixed * scale + lax.dot_general(
        v, weights.astype(jnp.bfloat16), (((0,), (0,)), ((), ())),
        preferred_element_type=jnp.float32,
    )
    return new_top, total, mixed


def device_place():
    group, seq = lax.axis_index("cand"), lax.axis_index("seq")
    return group // 2, group % 2, seq // 2, seq % 2


def prompt_kernel(layout, w, chunk, facts, own, other, *refs):
    q_out, mixed_ref, top_ref, total_ref, k_all, v_all = refs
    x, core, r, y = device_place()
    rows = k_all.shape[0] // (8 * layout.rings)
    queries = q_out.shape[1]
    first = own.shape[1] - 2 * layout.rings * rows
    for o, piece in enumerate((own, other)):
        for k in range(layout.rings):
            for d in range(4):
                group = (x ^ (d >> 1)) * 2 + (core ^ o)
                seq = lax.rem(r + layout.rings - k, layout.rings) * 2 + (y ^ (d & 1))
                at = pl.multiple_of((group * layout.rings * 2 + seq) * rows, rows)
                for half, target in enumerate((k_all, v_all)):
                    here = first + (half * layout.rings + k) * rows
                    target[pl.ds(at, rows), :] = piece[d, here : here + rows, :]
    for n in range(2):
        unit = unit_facts(facts, w, n)
        length, offset = unit[3], unit[4]

        @pl.when(r * (queries // GROUP) < length)
        def _():
            q_all = q_out.at[n]
            load_queries(unit, own, other, q_all)

            def run(at, size, state, masked):
                mask = None
                if masked:
                    place = lax.broadcasted_iota(jnp.int32, (size, queries), 0) + at
                    mask = place < offset
                return online_step(
                    q_all[...], k_all[pl.ds(at, size), :], v_all[pl.ds(at, size), :], mask, state
                )

            def whole(i, state):
                return run(pl.multiple_of(i * chunk, chunk), chunk, state, False)

            def part(i, state):
                return run(pl.multiple_of(i * (chunk // 2), chunk // 2), chunk // 2, state, True)

            state = (
                jnp.full((1, queries), LOWEST, jnp.float32),
                jnp.zeros((1, queries), jnp.float32),
                jnp.zeros((HEAD, queries), jnp.float32),
            )
            count = offset // chunk
            state = lax.fori_loop(0, count, whole, state)
            end = (offset + chunk // 2 - 1) // (chunk // 2)
            state = lax.fori_loop(count * 2, end, part, state)
            top_ref[n], total_ref[n], mixed_ref[n] = state


def query_places(first, swap, rows, queries):
    column = lax.broadcasted_iota(jnp.int32, (1, queries), 1)
    for g in range(GROUP - 1, 0, -1):
        column = jnp.where(column >= g * 2 * rows, column - g * 2 * rows, column)
    second = column >= rows
    row = jnp.where(second, column - rows, column)
    upper = jnp.where(second, 1 - swap, swap)
    return first + upper * rows + row


def response_kernel(layout, w, dx, facts, q_all, mixed, top, total, *refs):
    pieces = refs[: layout.rings]
    outs = refs[layout.rings : 2 + layout.rings]
    k_all, v_all = refs[2 + layout.rings :]
    _, _, r, y = device_place()
    rows = outs[0].shape[0]
    queries = q_all.shape[1]
    unit = unit_facts(facts, w, dx)
    length = unit[3]

    @pl.when(r * (2 * rows) >= length)
    def _():
        for out in outs:
            out[...] = jnp.zeros(out.shape, out.dtype)

    @pl.when(r * (2 * rows) < length)
    def _():
        for k, piece in enumerate(pieces):

            @pl.when(k <= r)
            def _():
                for dy in range(2):
                    at = pl.multiple_of(((r - k) * 2 + (y ^ dy)) * rows, rows)
                    k_all[pl.ds(at, rows), :] = piece[dx, dy, :, :HEAD]
                    v_all[pl.ds(at, rows), :] = piece[dx, dy, :, HEAD:]

        place = query_places(r * (2 * rows), y, rows, queries)
        top_ref, total_ref, mixed_ref = top.at[dx], total.at[dx], mixed.at[dx]
        half = 2 * rows

        def run(at, size, state):
            at = pl.multiple_of(at, half)
            key = lax.broadcasted_iota(jnp.int32, (size, queries), 0) + at
            mask = key <= jnp.minimum(place, length - 1)
            return online_step(
                q_all[dx], k_all[pl.ds(at, size), :], v_all[pl.ds(at, size), :], mask, state
            )

        last = jnp.minimum((r + 1) * half, length)
        count = (last + half - 1) // (2 * half)
        state = (top_ref[...], total_ref[...], mixed_ref[...])
        state = lax.fori_loop(
            0, count, lambda i, s: run(i * (2 * half), 2 * half, s), state
        )
        rest = (last - count * (2 * half) + half - 1) // half
        _, sums, result = lax.fori_loop(
            0, rest, lambda i, s: run(count * (2 * half), half, s), state
        )
        result = jnp.where(place < length, result * (1.0 / sums), 0.0).astype(jnp.bfloat16).T
        for dy, out in enumerate(outs):
            for g in range(GROUP):
                at = (g * 2 + dy) * rows
                out[:, g * HEAD : (g + 1) * HEAD] = result[at : at + rows]


def join_kernel(*refs):
    pieces, out = refs[:-1], refs[-1]
    own = own_head()
    for w in range(out.shape[0]):
        for d in range(4):
            lane = pl.ds(pl.multiple_of((own ^ d) * WIDE, HEAD), WIDE)
            out[w, :, lane] = pieces[w * 4 + d][...]


def divisor(total, *choices):
    for choice in choices:
        if total % choice == 0:
            return choice
    return total


def struct(*shape, dtype=jnp.bfloat16):
    return jax.ShapeDtypeStruct(shape, dtype)


def after(value, *others):
    return lax.optimization_barrier((value, *others))[0]


def body(layout, q, rk, rv, pk, pv, lengths, offsets, ranks):
    cands, rows = q.shape[0], q.shape[1]
    queries = 2 * rows * GROUP
    bf16 = functools.partial(pltpu.VMEM, dtype=jnp.bfloat16)

    def exchange(pieces, *held):
        got = layout.exchange(pieces)
        if held:
            got[0] = after(got[0], *held)
        own = kernel_call(
            stack_kernel, struct(4, *got[0].shape), got, name="stack", scalars=0
        )
        return own, layout.permute(own, core=1)

    facts = jnp.concatenate([lengths, offsets, ranks])
    anywhere = pl.BlockSpec(memory_space=pl.ANY)
    *keys, prompt = pl.pallas_call(
        pack_first_kernel,
        out_shape=[struct(cands * rows, 2 * HEAD)] * 4 + [struct(pk.shape[0], 2 * pk.shape[1])],
        in_specs=[anywhere] * 4,
        out_specs=[VMEM] * 5,
        scratch_shapes=[pltpu.SemaphoreType.DMA((2 + 8 * cands,))],
        compiler_params=pltpu.CompilerParams(vmem_limit_bytes=PACK_VMEM),
        name="pack_first",
    )(rk, rv, pk, pv)
    prompt = layout.spread(prompt)
    asked = kernel_call(
        pack_queries_kernel,
        [struct(cands * GROUP * rows, HEAD)] * 4,
        (q,),
        name="pack_queries",
        scalars=0,
    )
    keys[3] = after(keys[3], asked[0])
    prompt_rows = layout.rings * pk.shape[0]
    packed = kernel_call(
        functools.partial(pack_kernel, layout.rings),
        [struct(cands * GROUP * rows + 2 * prompt_rows, HEAD)] * 4,
        (*asked, pk, pv, *prompt[1:]),
        name="pack_queries_prompt",
        scalars=0,
    )
    keys, keys_other = exchange(keys, packed[0])
    slots = kernel_call(
        select_keys_kernel,
        [struct(2, 2, rows, 2 * HEAD)] * cands,
        (facts, keys, keys_other),
        name="select_keys",
    )
    pieces = [layout.spread(slots[0])]
    for w in range(1, cands):
        pieces.append(layout.spread(after(slots[w], pieces[0][1])))
    packed = exchange(packed, pieces[0][1], pieces[0][2])

    prompt_keys = 8 * prompt_rows
    response_keys = layout.rings * 2 * rows
    chunk = divisor(prompt_keys, 1024, 512, 256)
    states = []
    for w in range(cands):
        states.append(
            kernel_call(
                functools.partial(prompt_kernel, layout, w, chunk),
                [
                    struct(2, queries, HEAD),
                    struct(2, HEAD, queries, dtype=jnp.float32),
                    struct(2, 1, queries, dtype=jnp.float32),
                    struct(2, 1, queries, dtype=jnp.float32),
                ],
                (facts, *packed),
                scratch=[bf16((prompt_keys, HEAD))] * 2,
                cost=(8 * queries * prompt_keys * HEAD, 4 * prompt_keys * HEAD),
                name="prompt_part",
                spare=16 << 20,
            )
        )
    finished = []
    for w in range(cands):
        outs = [None] * 4
        for dx in (1, 0):
            outs[dx * 2], outs[dx * 2 + 1] = kernel_call(
                functools.partial(response_kernel, layout, w, dx),
                [struct(rows, WIDE)] * 2,
                (facts, *states[w], *pieces[w]),
                scratch=[bf16((response_keys, HEAD))] * 2,
                cost=(4 * queries * response_keys * HEAD, 2 * response_keys * HEAD),
                name="response_part",
                spare=12 << 20,
            )
        finished += layout.exchange(outs)
    return kernel_call(join_kernel, struct(*q.shape), finished, name="join_heads", scalars=0)


def solution(mesh):
    in_specs = (
        P("cand", "seq", None),
        P("cand", "seq", None),
        P("cand", "seq", None),
        P(("cand", "seq"), None),
        P(("cand", "seq"), None),
        P(),
        P(),
        P(),
    )
    return jax.shard_map(
        functools.partial(body, Layout(mesh)),
        mesh=mesh,
        in_specs=in_specs,
        out_specs=P("cand", "seq", None),
        check_vma=False,
    )
```

profile of v0, /device:TPU:16, one launch (start us, length us, event | category | flops | bytes accessed | tf_op | source)
XLA Modules:
  0.0 85.0 jit_solution(2764952610592124025)
XLA Ops:
  0.0 2.0 %pack_first.1 = (bf16[192,256]{1,0:T(8,128)(2,1)}, bf16[192,256]{1,0:T(8,128)(2,1)}, bf16[192,256]{1,0:T(8,128)(2,1)}, bf16[192,256]{1,0:T(8,128)(2,1)}, bf16[64,1024]{1,0:T(8,128)(2,1)}) custom-call(bf16[2,96,512]{2,1,0:T(8,128)(2,1)} %rk.1, bf16[2,96,512]{2,1,0:T(8,128)(2,1)} %rv.1, bf16[64,512]{1,0:T(8,128)(2,1)} %refs_4_.1, bf16[64,512]{1,0:T(8,128)(2,1)} %refs_5_.1), custom_call_target="tpu_custom_call" | custom-call | tf_op jit(solution)/shard_map/pack_first/pallas_call | solution.py:345
  2.0 1.6 %collective-permute-start = (bf16[64,1024]{1,0:T(8,128)(2,1)}, bf16[64,1024]{1,0:T(8,128)(2,1)S(1)}, u32[]{:S(2)}, u32[]{:S(2)}) collective-permute-start(bf16[64,1024]{1,0:T(8,128)(2,1)} %get-tuple-element.44), channel_id=1, source_target_pairs={{0,2},{1,3},{2,4},{3,5},{4,6},{5,7},{6,0},{7,1},{8,10},{9,11},{10,... | collective-permute-start | bytes 393224 | tf_op jit(solution)/shard_map/ppermute | solution.py:39
  5.2 1.7 %collective-permute-start.3 = (bf16[192,256]{1,0:T(8,128)(2,1)}, bf16[192,256]{1,0:T(8,128)(2,1)S(1)}, u32[]{:S(2)}, u32[]{:S(2)}) collective-permute-start(bf16[192,256]{1,0:T(8,128)(2,1)} %get-tuple-element.48), channel_id=1, source_target_pairs={{0,1},{1,0},{2,3},{3,2},{4,5},{5,4},{6,7},{7,6},{8,9},{9,8},{10,11... | collective-permute-start | bytes 294920 | tf_op jit(solution)/shard_map/ppermute | solution.py:39
  9.7 4.5 %collective-permute-done.refs_6_ = bf16[64,1024]{1,0:T(8,128)(2,1)S(1)} collective-permute-done((bf16[64,1024]{1,0:T(8,128)(2,1)}, bf16[64,1024]{1,0:T(8,128)(2,1)S(1)}, u32[]{:S(2)}, u32[]{:S(2)}) %collective-permute-start) | collective-permute-done | bytes 131104 | tf_op jit(solution)/shard_map/ppermute | solution.py:39
  14.3 2.4 %collective-permute-start.5 = (bf16[192,256]{1,0:T(8,128)(2,1)}, bf16[192,256]{1,0:T(8,128)(2,1)S(1)}, u32[]{:S(2)}, u32[]{:S(2)}) collective-permute-start(bf16[192,256]{1,0:T(8,128)(2,1)} %get-tuple-element.51), channel_id=1, source_target_pairs={{0,17},{1,16},{2,19},{3,18},{4,21},{5,20},{6,23},{7,22},{8,25},{9,... | collective-permute-start | bytes 294920 | tf_op jit(solution)/shard_map/ppermute | solution.py:39
  16.9 3.1 %collective-permute-done.5.refs_3_ = bf16[192,256]{1,0:T(8,128)(2,1)S(1)} collective-permute-done((bf16[192,256]{1,0:T(8,128)(2,1)}, bf16[192,256]{1,0:T(8,128)(2,1)S(1)}, u32[]{:S(2)}, u32[]{:S(2)}) %collective-permute-start.5) | collective-permute-done | bytes 98336 | tf_op jit(solution)/shard_map/ppermute | solution.py:39
  20.1 1.6 %collective-permute-start.9 = (bf16[1472,128]{1,0:T(8,128)(2,1)S(1)}, bf16[1472,128]{1,0:T(8,128)(2,1)S(1)}, u32[]{:S(2)}, u32[]{:S(2)}) collective-permute-start(bf16[1472,128]{1,0:T(8,128)(2,1)S(1)} %get-tuple-element.54), channel_id=1, source_target_pairs={{0,1},{1,0},{2,3},{3,2},{4,5},{5,4},{6,7},{7,6},{8,9},{9,8},{10,11... | collective-permute-start | bytes 1130504 | tf_op jit(solution)/shard_map/ppermute | solution.py:39
  21.7 1.5 %collective-permute-start.10 = (bf16[1472,128]{1,0:T(8,128)(2,1)S(1)}, bf16[1472,128]{1,0:T(8,128)(2,1)S(1)}, u32[]{:S(2)}, u32[]{:S(2)}) collective-permute-start(bf16[1472,128]{1,0:T(8,128)(2,1)S(1)} %get-tuple-element.55), channel_id=1, source_target_pairs={{0,16},{1,17},{2,18},{3,19},{4,20},{5,21},{6,22},{7,23},{8,24},{9,... | collective-permute-start | bytes 1130504 | tf_op jit(solution)/shard_map/ppermute | solution.py:39
  25.5 10.9 %collective-permute-done.7.refs_1_ = bf16[2,2,96,256]{3,2,1,0:T(8,128)(2,1)S(1)} collective-permute-done((bf16[2,2,96,256]{3,2,1,0:T(8,128)(2,1)S(1)}, bf16[2,2,96,256]{3,2,1,0:T(8,128)(2,1)S(1)}, u32[]{:S(2)}, u32[]{:S(2)}) %collective-permute-start.7) | collective-permute-done | bytes 196640 | tf_op jit(solution)/shard_map/ppermute | solution.py:39
  36.5 4.0 %collective-permute-done.11.refs_3_ = bf16[1472,128]{1,0:T(8,128)(2,1)S(1)} collective-permute-done((bf16[1472,128]{1,0:T(8,128)(2,1)S(1)}, bf16[1472,128]{1,0:T(8,128)(2,1)S(1)}, u32[]{:S(2)}, u32[]{:S(2)}) %collective-permute-start.11) | collective-permute-done | bytes 376864 | tf_op jit(solution)/shard_map/ppermute | solution.py:39
  40.8 2.0 %collective-permute-start.17 = (bf16[2,2,96,256]{3,2,1,0:T(8,128)(2,1)S(1)}, bf16[2,2,96,256]{3,2,1,0:T(8,128)(2,1)S(1)}, u32[]{:S(2)}, u32[]{:S(2)}) collective-permute-start(bf16[2,2,96,256]{3,2,1,0:T(8,128)(2,1)S(1)} %get-tuple-element.70.refs_0_), channel_id=1, source_target_pairs={{0,2},{1,3},{2,4},{3,5},{4,6},{5,7},{6,0},{7,1},{8,10},{9,11},{10,... | collective-permute-start | bytes 589832 | tf_op jit(solution)/shard_map/ppermute | solution.py:39
  43.4 2.9 %collective-permute-start.19 = (bf16[2,2,96,256]{3,2,1,0:T(8,128)(2,1)S(1)}, bf16[2,2,96,256]{3,2,1,0:T(8,128)(2,1)S(1)}, u32[]{:S(2)}, u32[]{:S(2)}) collective-permute-start(bf16[2,2,96,256]{3,2,1,0:T(8,128)(2,1)S(1)} %get-tuple-element.70.refs_0_), channel_id=1, source_target_pairs={{0,6},{1,7},{2,0},{3,1},{4,2},{5,3},{6,4},{7,5},{8,14},{9,15},{10,... | collective-permute-start | bytes 589832 | tf_op jit(solution)/shard_map/ppermute | solution.py:39
  46.3 7.4 %prompt_part.2 = (bf16[2,960,128]{2,1,0:T(8,128)(2,1)S(1)}, f32[2,128,960]{2,1,0:T(8,128)S(1)}, f32[2,1,960]{2,1,0:T(1,128)S(1)}, f32[2,1,960]{2,1,0:T(1,128)S(1)}) custom-call(s32[24]{0:T(128)S(1)} %pad_add_fusion.facts, bf16[4,1472,128]{2,1,0:T(8,128)(2,1)S(1)} %stack.3.own, bf16[4,1472,128]{2,1,0:T(8,128)(2,1)S(1)} %collective-permute-done.12.other), custom_call_target="tpu_custom_call" | custom-call | flops 2013265920 | bytes 1048576 | tf_op jit(solution)/shard_map/prompt_part/pallas_call | solution.py:58
  53.7 2.7 %response_part.4 = (bf16[96,640]{1,0:T(8,128)(2,1)S(1)}, bf16[96,640]{1,0:T(8,128)(2,1)S(1)}) custom-call(s32[24]{0:T(128)S(1)} %pad_add_fusion.facts, bf16[2,960,128]{2,1,0:T(8,128)(2,1)S(1)} %get-tuple-element.57.q_all, f32[2,128,960]{2,1,0:T(8,128)S(1)} %get-tuple-element.58.mixed, f32[2,1,960]{2,1,0:T(1,128)S(1)} %get-tuple-element.59.top, ...), custom_call_target="tpu_custom_call" | custom-call | flops 377487360 | bytes 196608 | tf_op jit(solution)/shard_map/response_part/pallas_call | solution.py:58
  56.3 1.6 %collective-permute-start.14 = (bf16[96,640]{1,0:T(8,128)(2,1)S(1)}, bf16[96,640]{1,0:T(8,128)(2,1)S(1)}, u32[]{:S(2)}, u32[]{:S(2)}) collective-permute-start(bf16[96,640]{1,0:T(8,128)(2,1)S(1)} %get-tuple-element.62), channel_id=1, source_target_pairs={{0,1},{1,0},{2,3},{3,2},{4,5},{5,4},{6,7},{7,6},{8,9},{9,8},{10,11... | collective-permute-start | bytes 368648 | tf_op jit(solution)/shard_map/ppermute | solution.py:39
  57.9 2.8 %response_part.5 = (bf16[96,640]{1,0:T(8,128)(2,1)S(1)}, bf16[96,640]{1,0:T(8,128)(2,1)S(1)}) custom-call(s32[24]{0:T(128)S(1)} %pad_add_fusion.facts, bf16[2,960,128]{2,1,0:T(8,128)(2,1)S(1)} %get-tuple-element.57.q_all, f32[2,128,960]{2,1,0:T(8,128)S(1)} %get-tuple-element.58.mixed, f32[2,1,960]{2,1,0:T(1,128)S(1)} %get-tuple-element.59.top, ...), custom_call_target="tpu_custom_call" | custom-call | flops 377487360 | bytes 196608 | tf_op jit(solution)/shard_map/response_part/pallas_call | solution.py:58
  60.8 1.6 %collective-permute-start.15 = (bf16[96,640]{1,0:T(8,128)(2,1)S(1)}, bf16[96,640]{1,0:T(8,128)(2,1)S(1)}, u32[]{:S(2)}, u32[]{:S(2)}) collective-permute-start(bf16[96,640]{1,0:T(8,128)(2,1)S(1)} %get-tuple-element.63), channel_id=1, source_target_pairs={{0,16},{1,17},{2,18},{3,19},{4,20},{5,21},{6,22},{7,23},{8,24},{9,... | collective-permute-start | bytes 368648 | tf_op jit(solution)/shard_map/ppermute | solution.py:39
  62.3 6.8 %prompt_part.3 = (bf16[2,960,128]{2,1,0:T(8,128)(2,1)S(1)}, f32[2,128,960]{2,1,0:T(8,128)S(1)}, f32[2,1,960]{2,1,0:T(1,128)S(1)}, f32[2,1,960]{2,1,0:T(1,128)S(1)}) custom-call(s32[24]{0:T(128)S(1)} %pad_add_fusion.facts, bf16[4,1472,128]{2,1,0:T(8,128)(2,1)S(1)} %stack.3.own, bf16[4,1472,128]{2,1,0:T(8,128)(2,1)S(1)} %collective-permute-done.12.other), custom_call_target="tpu_custom_call" | custom-call | flops 2013265920 | bytes 1048576 | tf_op jit(solution)/shard_map/prompt_part/pallas_call | solution.py:58
  69.7 2.7 %response_part.6 = (bf16[96,640]{1,0:T(8,128)(2,1)S(1)}, bf16[96,640]{1,0:T(8,128)(2,1)S(1)}) custom-call(s32[24]{0:T(128)S(1)} %pad_add_fusion.facts, bf16[2,960,128]{2,1,0:T(8,128)(2,1)S(1)} %get-tuple-element.65.q_all, f32[2,128,960]{2,1,0:T(8,128)S(1)} %get-tuple-element.66.mixed, f32[2,1,960]{2,1,0:T(1,128)S(1)} %get-tuple-element.67.top, ...), custom_call_target="tpu_custom_call" | custom-call | flops 377487360 | bytes 196608 | tf_op jit(solution)/shard_map/response_part/pallas_call | solution.py:58
  72.4 1.6 %collective-permute-start.20 = (bf16[96,640]{1,0:T(8,128)(2,1)S(1)}, bf16[96,640]{1,0:T(8,128)(2,1)S(1)}, u32[]{:S(2)}, u32[]{:S(2)}) collective-permute-start(bf16[96,640]{1,0:T(8,128)(2,1)S(1)} %get-tuple-element.72), channel_id=1, source_target_pairs={{0,1},{1,0},{2,3},{3,2},{4,5},{5,4},{6,7},{7,6},{8,9},{9,8},{10,11... | collective-permute-start | bytes 368648 | tf_op jit(solution)/shard_map/ppermute | solution.py:39
  74.0 2.7 %response_part.7 = (bf16[96,640]{1,0:T(8,128)(2,1)S(1)}, bf16[96,640]{1,0:T(8,128)(2,1)S(1)}) custom-call(s32[24]{0:T(128)S(1)} %pad_add_fusion.facts, bf16[2,960,128]{2,1,0:T(8,128)(2,1)S(1)} %get-tuple-element.65.q_all, f32[2,128,960]{2,1,0:T(8,128)S(1)} %get-tuple-element.66.mixed, f32[2,1,960]{2,1,0:T(1,128)S(1)} %get-tuple-element.67.top, ...), custom_call_target="tpu_custom_call" | custom-call | flops 377487360 | bytes 196608 | tf_op jit(solution)/shard_map/response_part/pallas_call | solution.py:58
  76.6 1.6 %collective-permute-start.21 = (bf16[96,640]{1,0:T(8,128)(2,1)S(1)}, bf16[96,640]{1,0:T(8,128)(2,1)S(1)}, u32[]{:S(2)}, u32[]{:S(2)}) collective-permute-start(bf16[96,640]{1,0:T(8,128)(2,1)S(1)} %get-tuple-element.73), channel_id=1, source_target_pairs={{0,16},{1,17},{2,18},{3,19},{4,20},{5,21},{6,22},{7,23},{8,24},{9,... | collective-permute-start | bytes 368648 | tf_op jit(solution)/shard_map/ppermute | solution.py:39
  78.7 2.9 %collective-permute-done.21.refs_6_ = bf16[96,640]{1,0:T(8,128)(2,1)S(1)} collective-permute-done((bf16[96,640]{1,0:T(8,128)(2,1)S(1)}, bf16[96,640]{1,0:T(8,128)(2,1)S(1)}, u32[]{:S(2)}, u32[]{:S(2)}) %collective-permute-start.21) | collective-permute-done | bytes 122912 | tf_op jit(solution)/shard_map/ppermute | solution.py:39
  81.6 2.4 %collective-permute-done.22.refs_7_ = bf16[96,640]{1,0:T(8,128)(2,1)S(1)} collective-permute-done((bf16[96,640]{1,0:T(8,128)(2,1)S(1)}, bf16[96,640]{1,0:T(8,128)(2,1)S(1)}, u32[]{:S(2)}, u32[]{:S(2)}) %collective-permute-start.22) | collective-permute-done | bytes 122912 | tf_op jit(solution)/shard_map/ppermute | solution.py:39
  (50 shorter events, 9.9 us)
Async XLA Ops:
  0.0 16.7 %copy-start.2 = (bf16[64,512]{1,0:T(8,128)(2,1)S(1)}, bf16[64,512]{1,0:T(8,128)(2,1)}, u32[]{:S(2)}) copy-start(bf16[64,512]{1,0:T(8,128)(2,1)} %refs_5_.1) | copy-start | bytes 196612
  2.0 12.3 %collective-permute-start = (bf16[64,1024]{1,0:T(8,128)(2,1)}, bf16[64,1024]{1,0:T(8,128)(2,1)S(1)}, u32[]{:S(2)}, u32[]{:S(2)}) collective-permute-start(bf16[64,1024]{1,0:T(8,128)(2,1)} %get-tuple-element.44), channel_id=1, source_target_pairs={{0,2},{1,3},{2,4},{3,5},{4,6},{5,7},{6,0},{7,1},{8,10},{9,11},{10,... | collective-permute-start | bytes 393224 | tf_op jit(solution)/shard_map/ppermute | solution.py:39
  3.6 13.1 %collective-permute-start.1 = (bf16[64,1024]{1,0:T(8,128)(2,1)}, bf16[64,1024]{1,0:T(8,128)(2,1)S(1)}, u32[]{:S(2)}, u32[]{:S(2)}) collective-permute-start(bf16[64,1024]{1,0:T(8,128)(2,1)} %get-tuple-element.44), channel_id=1, source_target_pairs={{0,4},{1,5},{2,6},{3,7},{4,0},{5,1},{6,2},{7,3},{8,12},{9,13},{10,... | collective-permute-start | bytes 393224 | tf_op jit(solution)/shard_map/ppermute | solution.py:39
  4.0 12.8 %collective-permute-start.2 = (bf16[64,1024]{1,0:T(8,128)(2,1)}, bf16[64,1024]{1,0:T(8,128)(2,1)S(1)}, u32[]{:S(2)}, u32[]{:S(2)}) collective-permute-start(bf16[64,1024]{1,0:T(8,128)(2,1)} %get-tuple-element.44), channel_id=1, source_target_pairs={{0,6},{1,7},{2,0},{3,1},{4,2},{5,3},{6,4},{7,5},{8,14},{9,15},{10,... | collective-permute-start | bytes 393224 | tf_op jit(solution)/shard_map/ppermute | solution.py:39
  5.2 11.8 %collective-permute-start.3 = (bf16[192,256]{1,0:T(8,128)(2,1)}, bf16[192,256]{1,0:T(8,128)(2,1)S(1)}, u32[]{:S(2)}, u32[]{:S(2)}) collective-permute-start(bf16[192,256]{1,0:T(8,128)(2,1)} %get-tuple-element.48), channel_id=1, source_target_pairs={{0,1},{1,0},{2,3},{3,2},{4,5},{5,4},{6,7},{7,6},{8,9},{9,8},{10,11... | collective-permute-start | bytes 294920 | tf_op jit(solution)/shard_map/ppermute | solution.py:39
  6.8 10.1 %collective-permute-start.4 = (bf16[192,256]{1,0:T(8,128)(2,1)}, bf16[192,256]{1,0:T(8,128)(2,1)S(1)}, u32[]{:S(2)}, u32[]{:S(2)}) collective-permute-start(bf16[192,256]{1,0:T(8,128)(2,1)} %get-tuple-element.49), channel_id=1, source_target_pairs={{0,16},{1,17},{2,18},{3,19},{4,20},{5,21},{6,22},{7,23},{8,24},{9,... | collective-permute-start | bytes 294920 | tf_op jit(solution)/shard_map/ppermute | solution.py:39
  14.3 5.7 %collective-permute-start.5 = (bf16[192,256]{1,0:T(8,128)(2,1)}, bf16[192,256]{1,0:T(8,128)(2,1)S(1)}, u32[]{:S(2)}, u32[]{:S(2)}) collective-permute-start(bf16[192,256]{1,0:T(8,128)(2,1)} %get-tuple-element.51), channel_id=1, source_target_pairs={{0,17},{1,16},{2,19},{3,18},{4,21},{5,20},{6,23},{7,22},{8,25},{9,... | collective-permute-start | bytes 294920 | tf_op jit(solution)/shard_map/ppermute | solution.py:39
  20.0 3.7 %collective-permute-start.6 = (bf16[4,192,256]{2,1,0:T(8,128)(2,1)S(1)}, bf16[4,192,256]{2,1,0:T(8,128)(2,1)S(1)}, u32[]{:S(2)}, u32[]{:S(2)}) collective-permute-start(bf16[4,192,256]{2,1,0:T(8,128)(2,1)S(1)} %stack.2.own), channel_id=1, source_target_pairs={{0,8},{1,9},{2,10},{3,11},{4,12},{5,13},{6,14},{7,15},{8,0},{9,1},... | collective-permute-start | bytes 1179656 | tf_op jit(solution)/shard_map/ppermute | solution.py:39
  20.1 16.4 %collective-permute-start.9 = (bf16[1472,128]{1,0:T(8,128)(2,1)S(1)}, bf16[1472,128]{1,0:T(8,128)(2,1)S(1)}, u32[]{:S(2)}, u32[]{:S(2)}) collective-permute-start(bf16[1472,128]{1,0:T(8,128)(2,1)S(1)} %get-tuple-element.54), channel_id=1, source_target_pairs={{0,1},{1,0},{2,3},{3,2},{4,5},{5,4},{6,7},{7,6},{8,9},{9,8},{10,11... | collective-permute-start | bytes 1130504 | tf_op jit(solution)/shard_map/ppermute | solution.py:39
  21.7 14.8 %collective-permute-start.10 = (bf16[1472,128]{1,0:T(8,128)(2,1)S(1)}, bf16[1472,128]{1,0:T(8,128)(2,1)S(1)}, u32[]{:S(2)}, u32[]{:S(2)}) collective-permute-start(bf16[1472,128]{1,0:T(8,128)(2,1)S(1)} %get-tuple-element.55), channel_id=1, source_target_pairs={{0,16},{1,17},{2,18},{3,19},{4,20},{5,21},{6,22},{7,23},{8,24},{9,... | collective-permute-start | bytes 1130504 | tf_op jit(solution)/shard_map/ppermute | solution.py:39
  23.2 17.4 %collective-permute-start.11 = (bf16[1472,128]{1,0:T(8,128)(2,1)S(1)}, bf16[1472,128]{1,0:T(8,128)(2,1)S(1)}, u32[]{:S(2)}, u32[]{:S(2)}) collective-permute-start(bf16[1472,128]{1,0:T(8,128)(2,1)S(1)} %get-tuple-element.56), channel_id=1, source_target_pairs={{0,17},{1,16},{2,19},{3,18},{4,21},{5,20},{6,23},{7,22},{8,25},{9,... | collective-permute-start | bytes 1130504 | tf_op jit(solution)/shard_map/ppermute | solution.py:39
  24.4 12.1 %collective-permute-start.7 = (bf16[2,2,96,256]{3,2,1,0:T(8,128)(2,1)S(1)}, bf16[2,2,96,256]{3,2,1,0:T(8,128)(2,1)S(1)}, u32[]{:S(2)}, u32[]{:S(2)}) collective-permute-start(bf16[2,2,96,256]{3,2,1,0:T(8,128)(2,1)S(1)} %get-tuple-element.52.refs_0_), channel_id=1, source_target_pairs={{0,2},{1,3},{2,4},{3,5},{4,6},{5,7},{6,0},{7,1},{8,10},{9,11},{10,... | collective-permute-start | bytes 589832 | tf_op jit(solution)/shard_map/ppermute | solution.py:39
  24.4 12.0 %collective-permute-start.8 = (bf16[2,2,96,256]{3,2,1,0:T(8,128)(2,1)S(1)}, bf16[2,2,96,256]{3,2,1,0:T(8,128)(2,1)S(1)}, u32[]{:S(2)}, u32[]{:S(2)}) collective-permute-start(bf16[2,2,96,256]{3,2,1,0:T(8,128)(2,1)S(1)} %get-tuple-element.52.refs_0_), channel_id=1, source_target_pairs={{0,4},{1,5},{2,6},{3,7},{4,0},{5,1},{6,2},{7,3},{8,12},{9,13},{10,... | collective-permute-start | bytes 589832 | tf_op jit(solution)/shard_map/ppermute | solution.py:39
  40.6 5.6 %collective-permute-start.12 = (bf16[4,1472,128]{2,1,0:T(8,128)(2,1)S(1)}, bf16[4,1472,128]{2,1,0:T(8,128)(2,1)S(1)}, u32[]{:S(2)}, u32[]{:S(2)}) collective-permute-start(bf16[4,1472,128]{2,1,0:T(8,128)(2,1)S(1)} %stack.3.own), channel_id=1, source_target_pairs={{0,8},{1,9},{2,10},{3,11},{4,12},{5,13},{6,14},{7,15},{8,0},{9,1},... | collective-permute-start | bytes 4521992 | tf_op jit(solution)/shard_map/ppermute | solution.py:39
  40.7 12.9 %collective-permute-start.13 = (bf16[2,2,96,256]{3,2,1,0:T(8,128)(2,1)S(1)}, bf16[2,2,96,256]{3,2,1,0:T(8,128)(2,1)S(1)}, u32[]{:S(2)}, u32[]{:S(2)}) collective-permute-start(bf16[2,2,96,256]{3,2,1,0:T(8,128)(2,1)S(1)} %get-tuple-element.52.refs_0_), channel_id=1, source_target_pairs={{0,6},{1,7},{2,0},{3,1},{4,2},{5,3},{6,4},{7,5},{8,14},{9,15},{10,... | collective-permute-start | bytes 589832 | tf_op jit(solution)/shard_map/ppermute | solution.py:39
  40.8 28.4 %collective-permute-start.17 = (bf16[2,2,96,256]{3,2,1,0:T(8,128)(2,1)S(1)}, bf16[2,2,96,256]{3,2,1,0:T(8,128)(2,1)S(1)}, u32[]{:S(2)}, u32[]{:S(2)}) collective-permute-start(bf16[2,2,96,256]{3,2,1,0:T(8,128)(2,1)S(1)} %get-tuple-element.70.refs_0_), channel_id=1, source_target_pairs={{0,2},{1,3},{2,4},{3,5},{4,6},{5,7},{6,0},{7,1},{8,10},{9,11},{10,... | collective-permute-start | bytes 589832 | tf_op jit(solution)/shard_map/ppermute | solution.py:39
  42.8 26.9 %collective-permute-start.18 = (bf16[2,2,96,256]{3,2,1,0:T(8,128)(2,1)S(1)}, bf16[2,2,96,256]{3,2,1,0:T(8,128)(2,1)S(1)}, u32[]{:S(2)}, u32[]{:S(2)}) collective-permute-start(bf16[2,2,96,256]{3,2,1,0:T(8,128)(2,1)S(1)} %get-tuple-element.70.refs_0_), channel_id=1, source_target_pairs={{0,4},{1,5},{2,6},{3,7},{4,0},{5,1},{6,2},{7,3},{8,12},{9,13},{10,... | collective-permute-start | bytes 589832 | tf_op jit(solution)/shard_map/ppermute | solution.py:39
  43.4 26.4 %collective-permute-start.19 = (bf16[2,2,96,256]{3,2,1,0:T(8,128)(2,1)S(1)}, bf16[2,2,96,256]{3,2,1,0:T(8,128)(2,1)S(1)}, u32[]{:S(2)}, u32[]{:S(2)}) collective-permute-start(bf16[2,2,96,256]{3,2,1,0:T(8,128)(2,1)S(1)} %get-tuple-element.70.refs_0_), channel_id=1, source_target_pairs={{0,6},{1,7},{2,0},{3,1},{4,2},{5,3},{6,4},{7,5},{8,14},{9,15},{10,... | collective-permute-start | bytes 589832 | tf_op jit(solution)/shard_map/ppermute | solution.py:39
  56.3 21.9 %collective-permute-start.14 = (bf16[96,640]{1,0:T(8,128)(2,1)S(1)}, bf16[96,640]{1,0:T(8,128)(2,1)S(1)}, u32[]{:S(2)}, u32[]{:S(2)}) collective-permute-start(bf16[96,640]{1,0:T(8,128)(2,1)S(1)} %get-tuple-element.62), channel_id=1, source_target_pairs={{0,1},{1,0},{2,3},{3,2},{4,5},{5,4},{6,7},{7,6},{8,9},{9,8},{10,11... | collective-permute-start | bytes 368648 | tf_op jit(solution)/shard_map/ppermute | solution.py:39
  60.8 17.9 %collective-permute-start.15 = (bf16[96,640]{1,0:T(8,128)(2,1)S(1)}, bf16[96,640]{1,0:T(8,128)(2,1)S(1)}, u32[]{:S(2)}, u32[]{:S(2)}) collective-permute-start(bf16[96,640]{1,0:T(8,128)(2,1)S(1)} %get-tuple-element.63), channel_id=1, source_target_pairs={{0,16},{1,17},{2,18},{3,19},{4,20},{5,21},{6,22},{7,23},{8,24},{9,... | collective-permute-start | bytes 368648 | tf_op jit(solution)/shard_map/ppermute | solution.py:39
  69.2 9.5 %collective-permute-start.16 = (bf16[96,640]{1,0:T(8,128)(2,1)S(1)}, bf16[96,640]{1,0:T(8,128)(2,1)S(1)}, u32[]{:S(2)}, u32[]{:S(2)}) collective-permute-start(bf16[96,640]{1,0:T(8,128)(2,1)S(1)} %get-tuple-element.64), channel_id=1, source_target_pairs={{0,17},{1,16},{2,19},{3,18},{4,21},{5,20},{6,23},{7,22},{8,25},{9,... | collective-permute-start | bytes 368648 | tf_op jit(solution)/shard_map/ppermute | solution.py:39
  72.4 6.3 %collective-permute-start.20 = (bf16[96,640]{1,0:T(8,128)(2,1)S(1)}, bf16[96,640]{1,0:T(8,128)(2,1)S(1)}, u32[]{:S(2)}, u32[]{:S(2)}) collective-permute-start(bf16[96,640]{1,0:T(8,128)(2,1)S(1)} %get-tuple-element.72), channel_id=1, source_target_pairs={{0,1},{1,0},{2,3},{3,2},{4,5},{5,4},{6,7},{7,6},{8,9},{9,8},{10,11... | collective-permute-start | bytes 368648 | tf_op jit(solution)/shard_map/ppermute | solution.py:39
  76.6 4.9 %collective-permute-start.21 = (bf16[96,640]{1,0:T(8,128)(2,1)S(1)}, bf16[96,640]{1,0:T(8,128)(2,1)S(1)}, u32[]{:S(2)}, u32[]{:S(2)}) collective-permute-start(bf16[96,640]{1,0:T(8,128)(2,1)S(1)} %get-tuple-element.73), channel_id=1, source_target_pairs={{0,16},{1,17},{2,18},{3,19},{4,20},{5,21},{6,22},{7,23},{8,24},{9,... | collective-permute-start | bytes 368648 | tf_op jit(solution)/shard_map/ppermute | solution.py:39
  78.2 5.8 %collective-permute-start.22 = (bf16[96,640]{1,0:T(8,128)(2,1)S(1)}, bf16[96,640]{1,0:T(8,128)(2,1)S(1)}, u32[]{:S(2)}, u32[]{:S(2)}) collective-permute-start(bf16[96,640]{1,0:T(8,128)(2,1)S(1)} %get-tuple-element.74), channel_id=1, source_target_pairs={{0,17},{1,16},{2,19},{3,18},{4,21},{5,20},{6,23},{7,22},{8,25},{9,... | collective-permute-start | bytes 368648 | tf_op jit(solution)/shard_map/ppermute | solution.py:39
  (6 other events, 70.8 us)
where the time goes:
time: 85 us
  Pallas kernels  29.2 us (34%)
  waiting for transfers between devices  27.9 us (33%)
  starting transfers between devices  26.5 us (31%)
  local copies, waits for them, and re-layouts  1.22 us (1%)
    ppermute x23, waiting for transfers between devices, permute(): return lax.ppermute(array, AXES, pairs)  27.9 us
    pallas_call x12, Pallas kernels, kernel_call(): pl.pallas_call(kernel, out_shape=out_shape, in_specs=[SMEM] * scalars + [...  27.2 us
    ppermute x23, starting transfers between devices, permute(): return lax.ppermute(array, AXES, pairs)  26.5 us
    pallas_call x1, Pallas kernels, body(): pl.pallas_call(pack_first_kernel, out_shape=[struct(cands * rows, 2 * HEA...  1.98 us
  transfers between devices with their start and end apart: 23, of which 6 were waited for; matrix products, arithmetic and copies ran while one was open for 0% of the time, Pallas kernels for 31%

commit v1 on v0

--- a/solution.py
+++ b/solution.py
@@ -222,8 +222,11 @@
             def whole(i, state):
                 return run(pl.multiple_of(i * chunk, chunk), chunk, state, False)
 
+            def most(i, state):
+                return run(pl.multiple_of(i * chunk, chunk), chunk, state, True)
+
             def part(i, state):
-                return run(pl.multiple_of(i * (chunk // 2), chunk // 2), chunk // 2, state, True)
+                return run(pl.multiple_of(i * chunk, chunk), chunk // 2, state, True)
 
             state = (
                 jnp.full((1, queries), LOWEST, jnp.float32),
@@ -232,8 +235,10 @@
             )
             count = offset // chunk
             state = lax.fori_loop(0, count, whole, state)
-            end = (offset + chunk // 2 - 1) // (chunk // 2)
-            state = lax.fori_loop(count * 2, end, part, state)
+            rest = offset - count * chunk
+            halves = (rest + chunk // 2 - 1) // (chunk // 2)
+            state = lax.fori_loop(count, count + halves // 2, most, state)
+            state = lax.fori_loop(count, count + halves % 2, part, state)
             top_ref[n], total_ref[n], mixed_ref[n] = state
 
 
@@ -376,9 +381,9 @@
         name="select_keys",
     )
     pieces = [layout.spread(slots[0])]
+    packed = exchange(packed, pieces[0][1], pieces[0][2])
     for w in range(1, cands):
-        pieces.append(layout.spread(after(slots[w], pieces[0][1])))
-    packed = exchange(packed, pieces[0][1], pieces[0][2])
+        pieces.append(layout.spread(after(slots[w], packed[0])))
 
     prompt_keys = 8 * prompt_rows
     response_keys = layout.rings * 2 * rows

time: 85 us -> 84.2 us (level)
  the two profiles are of different devices: /device:TPU:16 before, /device:TPU:0 now
where the time goes in v1:
time: 84.2 us; the launch traced here: 83.3 us
  starting transfers between devices  34.7 us (41%)
  Pallas kernels  25.3 us (30%)
  waiting for transfers between devices  21.9 us (26%)
  local copies, waits for them, and re-layouts  1.22 us (1%)
    ppermute x23, starting transfers between devices, permute(): return lax.ppermute(array, AXES, pairs)  34.7 us
    pallas_call x12, Pallas kernels, kernel_call(): pl.pallas_call(kernel, out_shape=out_shape, in_specs=[SMEM] * scalars + [...  23.3 us
    ppermute x23, waiting for transfers between devices, permute(): return lax.ppermute(array, AXES, pairs)  21.9 us
    pallas_call x1, Pallas kernels, body(): pl.pallas_call(pack_first_kernel, out_shape=[struct(cands * rows, 2 * HEA...  1.96 us
  transfers between devices with their start and end apart: 23, of which 7 were waited for; matrix products, arithmetic and copies ran while one was open for 0% of the time, Pallas kernels for 27%

profile of v1, /device:TPU:0, one launch (start us, length us, event | category | flops | bytes accessed | tf_op | source)
XLA Modules:
  0.0 83.3 jit_solution(194936078778555371)
XLA Ops:
  0.0 2.0 %pack_first.1 = (bf16[192,256]{1,0:T(8,128)(2,1)}, bf16[192,256]{1,0:T(8,128)(2,1)}, bf16[192,256]{1,0:T(8,128)(2,1)}, bf16[192,256]{1,0:T(8,128)(2,1)}, bf16[64,1024]{1,0:T(8,128)(2,1)}) custom-call(bf16[2,96,512]{2,1,0:T(8,128)(2,1)} %rk.1, bf16[2,96,512]{2,1,0:T(8,128)(2,1)} %rv.1, bf16[64,512]{1,0:T(8,128)(2,1)} %refs_4_.1, bf16[64,512]{1,0:T(8,128)(2,1)} %refs_5_.1), custom_call_target="tpu_custom_call" | custom-call | tf_op jit(solution)/shard_map/pack_first/pallas_call | solution.py:350
  2.0 3.1 %collective-permute-start = (bf16[64,1024]{1,0:T(8,128)(2,1)}, bf16[64,1024]{1,0:T(8,128)(2,1)S(1)}, u32[]{:S(2)}, u32[]{:S(2)}) collective-permute-start(bf16[64,1024]{1,0:T(8,128)(2,1)} %get-tuple-element.44), channel_id=1, source_target_pairs={{0,2},{1,3},{2,4},{3,5},{4,6},{5,7},{6,0},{7,1},{8,10},{9,11},{10,... | collective-permute-start | bytes 393224 | tf_op jit(solution)/shard_map/ppermute | solution.py:39
  5.1 2.6 %collective-permute-start.1 = (bf16[64,1024]{1,0:T(8,128)(2,1)}, bf16[64,1024]{1,0:T(8,128)(2,1)S(1)}, u32[]{:S(2)}, u32[]{:S(2)}) collective-permute-start(bf16[64,1024]{1,0:T(8,128)(2,1)} %get-tuple-element.44), channel_id=1, source_target_pairs={{0,4},{1,5},{2,6},{3,7},{4,0},{5,1},{6,2},{7,3},{8,12},{9,13},{10,... | collective-permute-start | bytes 393224 | tf_op jit(solution)/shard_map/ppermute | solution.py:39
  14.4 2.1 %collective-permute-done.1.refs_7_ = bf16[64,1024]{1,0:T(8,128)(2,1)S(1)} collective-permute-done((bf16[64,1024]{1,0:T(8,128)(2,1)}, bf16[64,1024]{1,0:T(8,128)(2,1)S(1)}, u32[]{:S(2)}, u32[]{:S(2)}) %collective-permute-start.1) | collective-permute-done | bytes 131104 | tf_op jit(solution)/shard_map/ppermute | solution.py:39
  16.7 2.5 %collective-permute-done.5.refs_3_ = bf16[192,256]{1,0:T(8,128)(2,1)S(1)} collective-permute-done((bf16[192,256]{1,0:T(8,128)(2,1)}, bf16[192,256]{1,0:T(8,128)(2,1)S(1)}, u32[]{:S(2)}, u32[]{:S(2)}) %collective-permute-start.5) | collective-permute-done | bytes 98336 | tf_op jit(solution)/shard_map/ppermute | solution.py:39
  20.9 2.0 %collective-permute-start.11 = (bf16[1472,128]{1,0:T(8,128)(2,1)S(1)}, bf16[1472,128]{1,0:T(8,128)(2,1)S(1)}, u32[]{:S(2)}, u32[]{:S(2)}) collective-permute-start(bf16[1472,128]{1,0:T(8,128)(2,1)S(1)} %get-tuple-element.56), channel_id=1, source_target_pairs={{0,17},{1,16},{2,19},{3,18},{4,21},{5,20},{6,23},{7,22},{8,25},{9,... | collective-permute-start | bytes 1130504 | tf_op jit(solution)/shard_map/ppermute | solution.py:39
  23.6 3.0 %collective-permute-start.7 = (bf16[2,2,96,256]{3,2,1,0:T(8,128)(2,1)S(1)}, bf16[2,2,96,256]{3,2,1,0:T(8,128)(2,1)S(1)}, u32[]{:S(2)}, u32[]{:S(2)}) collective-permute-start(bf16[2,2,96,256]{3,2,1,0:T(8,128)(2,1)S(1)} %get-tuple-element.52.refs_0_), channel_id=1, source_target_pairs={{0,2},{1,3},{2,4},{3,5},{4,6},{5,7},{6,0},{7,1},{8,10},{9,11},{10,... | collective-permute-start | bytes 589832 | tf_op jit(solution)/shard_map/ppermute | solution.py:39
  26.7 1.9 %collective-permute-start.8 = (bf16[2,2,96,256]{3,2,1,0:T(8,128)(2,1)S(1)}, bf16[2,2,96,256]{3,2,1,0:T(8,128)(2,1)S(1)}, u32[]{:S(2)}, u32[]{:S(2)}) collective-permute-start(bf16[2,2,96,256]{3,2,1,0:T(8,128)(2,1)S(1)} %get-tuple-element.52.refs_0_), channel_id=1, source_target_pairs={{0,4},{1,5},{2,6},{3,7},{4,0},{5,1},{6,2},{7,3},{8,12},{9,13},{10,... | collective-permute-start | bytes 589832 | tf_op jit(solution)/shard_map/ppermute | solution.py:39
  28.5 4.0 %collective-permute-done.7.refs_1_ = bf16[2,2,96,256]{3,2,1,0:T(8,128)(2,1)S(1)} collective-permute-done((bf16[2,2,96,256]{3,2,1,0:T(8,128)(2,1)S(1)}, bf16[2,2,96,256]{3,2,1,0:T(8,128)(2,1)S(1)}, u32[]{:S(2)}, u32[]{:S(2)}) %collective-permute-start.7) | collective-permute-done | bytes 196640 | tf_op jit(solution)/shard_map/ppermute | solution.py:39
  32.6 7.8 %collective-permute-done.8.refs_2_ = bf16[2,2,96,256]{3,2,1,0:T(8,128)(2,1)S(1)} collective-permute-done((bf16[2,2,96,256]{3,2,1,0:T(8,128)(2,1)S(1)}, bf16[2,2,96,256]{3,2,1,0:T(8,128)(2,1)S(1)}, u32[]{:S(2)}, u32[]{:S(2)}) %collective-permute-start.8) | collective-permute-done | bytes 196640 | tf_op jit(solution)/shard_map/ppermute | solution.py:39
  40.5 3.9 %collective-permute-start.13 = (bf16[2,2,96,256]{3,2,1,0:T(8,128)(2,1)S(1)}, bf16[2,2,96,256]{3,2,1,0:T(8,128)(2,1)S(1)}, u32[]{:S(2)}, u32[]{:S(2)}) collective-permute-start(bf16[2,2,96,256]{3,2,1,0:T(8,128)(2,1)S(1)} %get-tuple-element.52.refs_0_), channel_id=1, source_target_pairs={{0,6},{1,7},{2,0},{3,1},{4,2},{5,3},{6,4},{7,5},{8,14},{9,15},{10,... | collective-permute-start | bytes 589832 | tf_op jit(solution)/shard_map/ppermute | solution.py:39
  44.5 2.4 %collective-permute-start.18 = (bf16[2,2,96,256]{3,2,1,0:T(8,128)(2,1)S(1)}, bf16[2,2,96,256]{3,2,1,0:T(8,128)(2,1)S(1)}, u32[]{:S(2)}, u32[]{:S(2)}) collective-permute-start(bf16[2,2,96,256]{3,2,1,0:T(8,128)(2,1)S(1)} %get-tuple-element.70.refs_0_), channel_id=1, source_target_pairs={{0,4},{1,5},{2,6},{3,7},{4,0},{5,1},{6,2},{7,3},{8,12},{9,13},{10,... | collective-permute-start | bytes 589832 | tf_op jit(solution)/shard_map/ppermute | solution.py:39
  48.3 6.8 %prompt_part.2 = (bf16[2,960,128]{2,1,0:T(8,128)(2,1)S(1)}, f32[2,128,960]{2,1,0:T(8,128)S(1)}, f32[2,1,960]{2,1,0:T(1,128)S(1)}, f32[2,1,960]{2,1,0:T(1,128)S(1)}) custom-call(s32[24]{0:T(128)S(1)} %pad_add_fusion.facts, bf16[4,1472,128]{2,1,0:T(8,128)(2,1)S(1)} %stack.3.own, bf16[4,1472,128]{2,1,0:T(8,128)(2,1)S(1)} %collective-permute-done.12.other), custom_call_target="tpu_custom_call" | custom-call | flops 2013265920 | bytes 1048576 | tf_op jit(solution)/shard_map/prompt_part/pallas_call | solution.py:58
  55.2 1.7 %response_part.4 = (bf16[96,640]{1,0:T(8,128)(2,1)S(1)}, bf16[96,640]{1,0:T(8,128)(2,1)S(1)}) custom-call(s32[24]{0:T(128)S(1)} %pad_add_fusion.facts, bf16[2,960,128]{2,1,0:T(8,128)(2,1)S(1)} %get-tuple-element.57.q_all, f32[2,128,960]{2,1,0:T(8,128)S(1)} %get-tuple-element.58.mixed, f32[2,1,960]{2,1,0:T(1,128)S(1)} %get-tuple-element.59.top, ...), custom_call_target="tpu_custom_call" | custom-call | flops 377487360 | bytes 196608 | tf_op jit(solution)/shard_map/response_part/pallas_call | solution.py:58
  56.9 1.6 %collective-permute-start.14 = (bf16[96,640]{1,0:T(8,128)(2,1)S(1)}, bf16[96,640]{1,0:T(8,128)(2,1)S(1)}, u32[]{:S(2)}, u32[]{:S(2)}) collective-permute-start(bf16[96,640]{1,0:T(8,128)(2,1)S(1)} %get-tuple-element.62), channel_id=1, source_target_pairs={{0,1},{1,0},{2,3},{3,2},{4,5},{5,4},{6,7},{7,6},{8,9},{9,8},{10,11... | collective-permute-start | bytes 368648 | tf_op jit(solution)/shard_map/ppermute | solution.py:39
  58.5 1.6 %response_part.5 = (bf16[96,640]{1,0:T(8,128)(2,1)S(1)}, bf16[96,640]{1,0:T(8,128)(2,1)S(1)}) custom-call(s32[24]{0:T(128)S(1)} %pad_add_fusion.facts, bf16[2,960,128]{2,1,0:T(8,128)(2,1)S(1)} %get-tuple-element.57.q_all, f32[2,128,960]{2,1,0:T(8,128)S(1)} %get-tuple-element.58.mixed, f32[2,1,960]{2,1,0:T(1,128)S(1)} %get-tuple-element.59.top, ...), custom_call_target="tpu_custom_call" | custom-call | flops 377487360 | bytes 196608 | tf_op jit(solution)/shard_map/response_part/pallas_call | solution.py:58
  60.1 1.6 %collective-permute-start.15 = (bf16[96,640]{1,0:T(8,128)(2,1)S(1)}, bf16[96,640]{1,0:T(8,128)(2,1)S(1)}, u32[]{:S(2)}, u32[]{:S(2)}) collective-permute-start(bf16[96,640]{1,0:T(8,128)(2,1)S(1)} %get-tuple-element.63), channel_id=1, source_target_pairs={{0,16},{1,17},{2,18},{3,19},{4,20},{5,21},{6,22},{7,23},{8,24},{9,... | collective-permute-start | bytes 368648 | tf_op jit(solution)/shard_map/ppermute | solution.py:39
  61.6 7.8 %prompt_part.3 = (bf16[2,960,128]{2,1,0:T(8,128)(2,1)S(1)}, f32[2,128,960]{2,1,0:T(8,128)S(1)}, f32[2,1,960]{2,1,0:T(1,128)S(1)}, f32[2,1,960]{2,1,0:T(1,128)S(1)}) custom-call(s32[24]{0:T(128)S(1)} %pad_add_fusion.facts, bf16[4,1472,128]{2,1,0:T(8,128)(2,1)S(1)} %stack.3.own, bf16[4,1472,128]{2,1,0:T(8,128)(2,1)S(1)} %collective-permute-done.12.other), custom_call_target="tpu_custom_call" | custom-call | flops 2013265920 | bytes 1048576 | tf_op jit(solution)/shard_map/prompt_part/pallas_call | solution.py:58
  70.0 1.6 %response_part.6 = (bf16[96,640]{1,0:T(8,128)(2,1)S(1)}, bf16[96,640]{1,0:T(8,128)(2,1)S(1)}) custom-call(s32[24]{0:T(128)S(1)} %pad_add_fusion.facts, bf16[2,960,128]{2,1,0:T(8,128)(2,1)S(1)} %get-tuple-element.65.q_all, f32[2,128,960]{2,1,0:T(8,128)S(1)} %get-tuple-element.66.mixed, f32[2,1,960]{2,1,0:T(1,128)S(1)} %get-tuple-element.67.top, ...), custom_call_target="tpu_custom_call" | custom-call | flops 377487360 | bytes 196608 | tf_op jit(solution)/shard_map/response_part/pallas_call | solution.py:58
  71.6 1.6 %collective-permute-start.20 = (bf16[96,640]{1,0:T(8,128)(2,1)S(1)}, bf16[96,640]{1,0:T(8,128)(2,1)S(1)}, u32[]{:S(2)}, u32[]{:S(2)}) collective-permute-start(bf16[96,640]{1,0:T(8,128)(2,1)S(1)} %get-tuple-element.72), channel_id=1, source_target_pairs={{0,1},{1,0},{2,3},{3,2},{4,5},{5,4},{6,7},{7,6},{8,9},{9,8},{10,11... | collective-permute-start | bytes 368648 | tf_op jit(solution)/shard_map/ppermute | solution.py:39
  73.2 1.6 %response_part.7 = (bf16[96,640]{1,0:T(8,128)(2,1)S(1)}, bf16[96,640]{1,0:T(8,128)(2,1)S(1)}) custom-call(s32[24]{0:T(128)S(1)} %pad_add_fusion.facts, bf16[2,960,128]{2,1,0:T(8,128)(2,1)S(1)} %get-tuple-element.65.q_all, f32[2,128,960]{2,1,0:T(8,128)S(1)} %get-tuple-element.66.mixed, f32[2,1,960]{2,1,0:T(1,128)S(1)} %get-tuple-element.67.top, ...), custom_call_target="tpu_custom_call" | custom-call | flops 377487360 | bytes 196608 | tf_op jit(solution)/shard_map/response_part/pallas_call | solution.py:58
  74.7 1.6 %collective-permute-start.21 = (bf16[96,640]{1,0:T(8,128)(2,1)S(1)}, bf16[96,640]{1,0:T(8,128)(2,1)S(1)}, u32[]{:S(2)}, u32[]{:S(2)}) collective-permute-start(bf16[96,640]{1,0:T(8,128)(2,1)S(1)} %get-tuple-element.73), channel_id=1, source_target_pairs={{0,16},{1,17},{2,18},{3,19},{4,20},{5,21},{6,22},{7,23},{8,24},{9,... | collective-permute-start | bytes 368648 | tf_op jit(solution)/shard_map/ppermute | solution.py:39
  77.9 2.5 %collective-permute-done.21.refs_6_ = bf16[96,640]{1,0:T(8,128)(2,1)S(1)} collective-permute-done((bf16[96,640]{1,0:T(8,128)(2,1)S(1)}, bf16[96,640]{1,0:T(8,128)(2,1)S(1)}, u32[]{:S(2)}, u32[]{:S(2)}) %collective-permute-start.21) | collective-permute-done | bytes 122912 | tf_op jit(solution)/shard_map/ppermute | solution.py:39
  80.4 1.9 %collective-permute-done.22.refs_7_ = bf16[96,640]{1,0:T(8,128)(2,1)S(1)} collective-permute-done((bf16[96,640]{1,0:T(8,128)(2,1)S(1)}, bf16[96,640]{1,0:T(8,128)(2,1)S(1)}, u32[]{:S(2)}, u32[]{:S(2)}) %collective-permute-start.22) | collective-permute-done | bytes 122912 | tf_op jit(solution)/shard_map/ppermute | solution.py:39
  (50 shorter events, 14.2 us)
Async XLA Ops:
  0.0 16.5 %copy-start.2 = (bf16[64,512]{1,0:T(8,128)(2,1)S(1)}, bf16[64,512]{1,0:T(8,128)(2,1)}, u32[]{:S(2)}) copy-start(bf16[64,512]{1,0:T(8,128)(2,1)} %refs_5_.1) | copy-start | bytes 196612
  2.0 11.5 %collective-permute-start = (bf16[64,1024]{1,0:T(8,128)(2,1)}, bf16[64,1024]{1,0:T(8,128)(2,1)S(1)}, u32[]{:S(2)}, u32[]{:S(2)}) collective-permute-start(bf16[64,1024]{1,0:T(8,128)(2,1)} %get-tuple-element.44), channel_id=1, source_target_pairs={{0,2},{1,3},{2,4},{3,5},{4,6},{5,7},{6,0},{7,1},{8,10},{9,11},{10,... | collective-permute-start | bytes 393224 | tf_op jit(solution)/shard_map/ppermute | solution.py:39
  5.1 11.4 %collective-permute-start.1 = (bf16[64,1024]{1,0:T(8,128)(2,1)}, bf16[64,1024]{1,0:T(8,128)(2,1)S(1)}, u32[]{:S(2)}, u32[]{:S(2)}) collective-permute-start(bf16[64,1024]{1,0:T(8,128)(2,1)} %get-tuple-element.44), channel_id=1, source_target_pairs={{0,4},{1,5},{2,6},{3,7},{4,0},{5,1},{6,2},{7,3},{8,12},{9,13},{10,... | collective-permute-start | bytes 393224 | tf_op jit(solution)/shard_map/ppermute | solution.py:39
  7.7 8.9 %collective-permute-start.2 = (bf16[64,1024]{1,0:T(8,128)(2,1)}, bf16[64,1024]{1,0:T(8,128)(2,1)S(1)}, u32[]{:S(2)}, u32[]{:S(2)}) collective-permute-start(bf16[64,1024]{1,0:T(8,128)(2,1)} %get-tuple-element.44), channel_id=1, source_target_pairs={{0,6},{1,7},{2,0},{3,1},{4,2},{5,3},{6,4},{7,5},{8,14},{9,15},{10,... | collective-permute-start | bytes 393224 | tf_op jit(solution)/shard_map/ppermute | solution.py:39
  9.0 7.7 %collective-permute-start.3 = (bf16[192,256]{1,0:T(8,128)(2,1)}, bf16[192,256]{1,0:T(8,128)(2,1)S(1)}, u32[]{:S(2)}, u32[]{:S(2)}) collective-permute-start(bf16[192,256]{1,0:T(8,128)(2,1)} %get-tuple-element.48), channel_id=1, source_target_pairs={{0,1},{1,0},{2,3},{3,2},{4,5},{5,4},{6,7},{7,6},{8,9},{9,8},{10,11... | collective-permute-start | bytes 294920 | tf_op jit(solution)/shard_map/ppermute | solution.py:39
  10.5 6.2 %collective-permute-start.4 = (bf16[192,256]{1,0:T(8,128)(2,1)}, bf16[192,256]{1,0:T(8,128)(2,1)S(1)}, u32[]{:S(2)}, u32[]{:S(2)}) collective-permute-start(bf16[192,256]{1,0:T(8,128)(2,1)} %get-tuple-element.49), channel_id=1, source_target_pairs={{0,16},{1,17},{2,18},{3,19},{4,20},{5,21},{6,22},{7,23},{8,24},{9,... | collective-permute-start | bytes 294920 | tf_op jit(solution)/shard_map/ppermute | solution.py:39
  13.4 5.8 %collective-permute-start.5 = (bf16[192,256]{1,0:T(8,128)(2,1)}, bf16[192,256]{1,0:T(8,128)(2,1)S(1)}, u32[]{:S(2)}, u32[]{:S(2)}) collective-permute-start(bf16[192,256]{1,0:T(8,128)(2,1)} %get-tuple-element.51), channel_id=1, source_target_pairs={{0,17},{1,16},{2,19},{3,18},{4,21},{5,20},{6,23},{7,22},{8,25},{9,... | collective-permute-start | bytes 294920 | tf_op jit(solution)/shard_map/ppermute | solution.py:39
  19.3 3.7 %collective-permute-start.6 = (bf16[4,192,256]{2,1,0:T(8,128)(2,1)S(1)}, bf16[4,192,256]{2,1,0:T(8,128)(2,1)S(1)}, u32[]{:S(2)}, u32[]{:S(2)}) collective-permute-start(bf16[4,192,256]{2,1,0:T(8,128)(2,1)S(1)} %stack.2.own), channel_id=1, source_target_pairs={{0,8},{1,9},{2,10},{3,11},{4,12},{5,13},{6,14},{7,15},{8,0},{9,1},... | collective-permute-start | bytes 1179656 | tf_op jit(solution)/shard_map/ppermute | solution.py:39
  19.3 21.0 %collective-permute-start.9 = (bf16[1472,128]{1,0:T(8,128)(2,1)S(1)}, bf16[1472,128]{1,0:T(8,128)(2,1)S(1)}, u32[]{:S(2)}, u32[]{:S(2)}) collective-permute-start(bf16[1472,128]{1,0:T(8,128)(2,1)S(1)} %get-tuple-element.54), channel_id=1, source_target_pairs={{0,1},{1,0},{2,3},{3,2},{4,5},{5,4},{6,7},{7,6},{8,9},{9,8},{10,11... | collective-permute-start | bytes 1130504 | tf_op jit(solution)/shard_map/ppermute | solution.py:39
  19.9 20.4 %collective-permute-start.10 = (bf16[1472,128]{1,0:T(8,128)(2,1)S(1)}, bf16[1472,128]{1,0:T(8,128)(2,1)S(1)}, u32[]{:S(2)}, u32[]{:S(2)}) collective-permute-start(bf16[1472,128]{1,0:T(8,128)(2,1)S(1)} %get-tuple-element.55), channel_id=1, source_target_pairs={{0,16},{1,17},{2,18},{3,19},{4,20},{5,21},{6,22},{7,23},{8,24},{9,... | collective-permute-start | bytes 1130504 | tf_op jit(solution)/shard_map/ppermute | solution.py:39
  20.9 19.4 %collective-permute-start.11 = (bf16[1472,128]{1,0:T(8,128)(2,1)S(1)}, bf16[1472,128]{1,0:T(8,128)(2,1)S(1)}, u32[]{:S(2)}, u32[]{:S(2)}) collective-permute-start(bf16[1472,128]{1,0:T(8,128)(2,1)S(1)} %get-tuple-element.56), channel_id=1, source_target_pairs={{0,17},{1,16},{2,19},{3,18},{4,21},{5,20},{6,23},{7,22},{8,25},{9,... | collective-permute-start | bytes 1130504 | tf_op jit(solution)/shard_map/ppermute | solution.py:39
  23.6 8.9 %collective-permute-start.7 = (bf16[2,2,96,256]{3,2,1,0:T(8,128)(2,1)S(1)}, bf16[2,2,96,256]{3,2,1,0:T(8,128)(2,1)S(1)}, u32[]{:S(2)}, u32[]{:S(2)}) collective-permute-start(bf16[2,2,96,256]{3,2,1,0:T(8,128)(2,1)S(1)} %get-tuple-element.52.refs_0_), channel_id=1, source_target_pairs={{0,2},{1,3},{2,4},{3,5},{4,6},{5,7},{6,0},{7,1},{8,10},{9,11},{10,... | collective-permute-start | bytes 589832 | tf_op jit(solution)/shard_map/ppermute | solution.py:39
  26.7 13.7 %collective-permute-start.8 = (bf16[2,2,96,256]{3,2,1,0:T(8,128)(2,1)S(1)}, bf16[2,2,96,256]{3,2,1,0:T(8,128)(2,1)S(1)}, u32[]{:S(2)}, u32[]{:S(2)}) collective-permute-start(bf16[2,2,96,256]{3,2,1,0:T(8,128)(2,1)S(1)} %get-tuple-element.52.refs_0_), channel_id=1, source_target_pairs={{0,4},{1,5},{2,6},{3,7},{4,0},{5,1},{6,2},{7,3},{8,12},{9,13},{10,... | collective-permute-start | bytes 589832 | tf_op jit(solution)/shard_map/ppermute | solution.py:39
  40.4 7.8 %collective-permute-start.12 = (bf16[4,1472,128]{2,1,0:T(8,128)(2,1)S(1)}, bf16[4,1472,128]{2,1,0:T(8,128)(2,1)S(1)}, u32[]{:S(2)}, u32[]{:S(2)}) collective-permute-start(bf16[4,1472,128]{2,1,0:T(8,128)(2,1)S(1)} %stack.3.own), channel_id=1, source_target_pairs={{0,8},{1,9},{2,10},{3,11},{4,12},{5,13},{6,14},{7,15},{8,0},{9,1},... | collective-permute-start | bytes 4521992 | tf_op jit(solution)/shard_map/ppermute | solution.py:39
  40.5 14.6 %collective-permute-start.13 = (bf16[2,2,96,256]{3,2,1,0:T(8,128)(2,1)S(1)}, bf16[2,2,96,256]{3,2,1,0:T(8,128)(2,1)S(1)}, u32[]{:S(2)}, u32[]{:S(2)}) collective-permute-start(bf16[2,2,96,256]{3,2,1,0:T(8,128)(2,1)S(1)} %get-tuple-element.52.refs_0_), channel_id=1, source_target_pairs={{0,6},{1,7},{2,0},{3,1},{4,2},{5,3},{6,4},{7,5},{8,14},{9,15},{10,... | collective-permute-start | bytes 589832 | tf_op jit(solution)/shard_map/ppermute | solution.py:39
  44.5 25.0 %collective-permute-start.17 = (bf16[2,2,96,256]{3,2,1,0:T(8,128)(2,1)S(1)}, bf16[2,2,96,256]{3,2,1,0:T(8,128)(2,1)S(1)}, u32[]{:S(2)}, u32[]{:S(2)}) collective-permute-start(bf16[2,2,96,256]{3,2,1,0:T(8,128)(2,1)S(1)} %get-tuple-element.70.refs_0_), channel_id=1, source_target_pairs={{0,2},{1,3},{2,4},{3,5},{4,6},{5,7},{6,0},{7,1},{8,10},{9,11},{10,... | collective-permute-start | bytes 589832 | tf_op jit(solution)/shard_map/ppermute | solution.py:39
  44.5 25.6 %collective-permute-start.18 = (bf16[2,2,96,256]{3,2,1,0:T(8,128)(2,1)S(1)}, bf16[2,2,96,256]{3,2,1,0:T(8,128)(2,1)S(1)}, u32[]{:S(2)}, u32[]{:S(2)}) collective-permute-start(bf16[2,2,96,256]{3,2,1,0:T(8,128)(2,1)S(1)} %get-tuple-element.70.refs_0_), channel_id=1, source_target_pairs={{0,4},{1,5},{2,6},{3,7},{4,0},{5,1},{6,2},{7,3},{8,12},{9,13},{10,... | collective-permute-start | bytes 589832 | tf_op jit(solution)/shard_map/ppermute | solution.py:39
  46.8 23.2 %collective-permute-start.19 = (bf16[2,2,96,256]{3,2,1,0:T(8,128)(2,1)S(1)}, bf16[2,2,96,256]{3,2,1,0:T(8,128)(2,1)S(1)}, u32[]{:S(2)}, u32[]{:S(2)}) collective-permute-start(bf16[2,2,96,256]{3,2,1,0:T(8,128)(2,1)S(1)} %get-tuple-element.70.refs_0_), channel_id=1, source_target_pairs={{0,6},{1,7},{2,0},{3,1},{4,2},{5,3},{6,4},{7,5},{8,14},{9,15},{10,... | collective-permute-start | bytes 589832 | tf_op jit(solution)/shard_map/ppermute | solution.py:39
  56.9 19.4 %collective-permute-start.14 = (bf16[96,640]{1,0:T(8,128)(2,1)S(1)}, bf16[96,640]{1,0:T(8,128)(2,1)S(1)}, u32[]{:S(2)}, u32[]{:S(2)}) collective-permute-start(bf16[96,640]{1,0:T(8,128)(2,1)S(1)} %get-tuple-element.62), channel_id=1, source_target_pairs={{0,1},{1,0},{2,3},{3,2},{4,5},{5,4},{6,7},{7,6},{8,9},{9,8},{10,11... | collective-permute-start | bytes 368648 | tf_op jit(solution)/shard_map/ppermute | solution.py:39
  60.1 16.7 %collective-permute-start.15 = (bf16[96,640]{1,0:T(8,128)(2,1)S(1)}, bf16[96,640]{1,0:T(8,128)(2,1)S(1)}, u32[]{:S(2)}, u32[]{:S(2)}) collective-permute-start(bf16[96,640]{1,0:T(8,128)(2,1)S(1)} %get-tuple-element.63), channel_id=1, source_target_pairs={{0,16},{1,17},{2,18},{3,19},{4,20},{5,21},{6,22},{7,23},{8,24},{9,... | collective-permute-start | bytes 368648 | tf_op jit(solution)/shard_map/ppermute | solution.py:39
  69.5 7.3 %collective-permute-start.16 = (bf16[96,640]{1,0:T(8,128)(2,1)S(1)}, bf16[96,640]{1,0:T(8,128)(2,1)S(1)}, u32[]{:S(2)}, u32[]{:S(2)}) collective-permute-start(bf16[96,640]{1,0:T(8,128)(2,1)S(1)} %get-tuple-element.64), channel_id=1, source_target_pairs={{0,17},{1,16},{2,19},{3,18},{4,21},{5,20},{6,23},{7,22},{8,25},{9,... | collective-permute-start | bytes 368648 | tf_op jit(solution)/shard_map/ppermute | solution.py:39
  71.6 6.3 %collective-permute-start.20 = (bf16[96,640]{1,0:T(8,128)(2,1)S(1)}, bf16[96,640]{1,0:T(8,128)(2,1)S(1)}, u32[]{:S(2)}, u32[]{:S(2)}) collective-permute-start(bf16[96,640]{1,0:T(8,128)(2,1)S(1)} %get-tuple-element.72), channel_id=1, source_target_pairs={{0,1},{1,0},{2,3},{3,2},{4,5},{5,4},{6,7},{7,6},{8,9},{9,8},{10,11... | collective-permute-start | bytes 368648 | tf_op jit(solution)/shard_map/ppermute | solution.py:39
  74.7 5.6 %collective-permute-start.21 = (bf16[96,640]{1,0:T(8,128)(2,1)S(1)}, bf16[96,640]{1,0:T(8,128)(2,1)S(1)}, u32[]{:S(2)}, u32[]{:S(2)}) collective-permute-start(bf16[96,640]{1,0:T(8,128)(2,1)S(1)} %get-tuple-element.73), channel_id=1, source_target_pairs={{0,16},{1,17},{2,18},{3,19},{4,20},{5,21},{6,22},{7,23},{8,24},{9,... | collective-permute-start | bytes 368648 | tf_op jit(solution)/shard_map/ppermute | solution.py:39
  76.3 6.0 %collective-permute-start.22 = (bf16[96,640]{1,0:T(8,128)(2,1)S(1)}, bf16[96,640]{1,0:T(8,128)(2,1)S(1)}, u32[]{:S(2)}, u32[]{:S(2)}) collective-permute-start(bf16[96,640]{1,0:T(8,128)(2,1)S(1)} %get-tuple-element.74), channel_id=1, source_target_pairs={{0,17},{1,16},{2,19},{3,18},{4,21},{5,20},{6,23},{7,22},{8,25},{9,... | collective-permute-start | bytes 368648 | tf_op jit(solution)/shard_map/ppermute | solution.py:39
  (6 other events, 52.8 us)
